TPU v7x, 32 devices: a whole 2x2x4 slice. The times are simulated.
32 devices in a mesh: dp: 8 (over y, x, core), tensor: 4 (over z).
Axes of the slice: x: 2, y: 2, z: 4, core: 2. Of those that a mesh axis runs over, the one named last changes fastest.
Arguments:
- target: bfloat16 [8192, 768], P('dp'), may hold values from -6 to 6
- memory: bfloat16 [8192, 768], P('dp'), may hold values from -6 to 6
- target_segments: int32 [8, 1024], P('dp'), may hold values from 0 to 4, as said below
- memory_segments: int32 [8, 1024], P('dp'), may hold values from 0 to 4, as said below
- self_query: bfloat16 [768, 768], P(None, 'tensor'), may hold values from -0.21875 to 0.21875
- self_query_bias: float32 [768], P('tensor'), may hold values from -3 to 3
- self_key: bfloat16 [768, 768], P(None, 'tensor'), may hold values from -0.21875 to 0.21875
- self_value: bfloat16 [768, 768], P(None, 'tensor'), may hold values from -0.21875 to 0.21875
- self_value_bias: float32 [768], P('tensor'), may hold values from -3 to 3
- self_output: bfloat16 [768, 768], P('tensor'), may hold values from -1.25 to 1.25
- self_output_bias: float32 [768], replicated, may hold values from -2 to 2
- first_gain: float32 [768], replicated, may hold values from 0.25 to 1.75
- first_shift: float32 [768], replicated, may hold values from -2 to 2
- cross_query: bfloat16 [768, 768], P(None, 'tensor'), may hold values from -0.21875 to 0.21875
- cross_query_bias: float32 [768], P('tensor'), may hold values from -3 to 3
- cross_key: bfloat16 [768, 768], P(None, 'tensor'), may hold values from -0.21875 to 0.21875
- cross_value: bfloat16 [768, 768], P(None, 'tensor'), may hold values from -0.21875 to 0.21875
- cross_value_bias: float32 [768], P('tensor'), may hold values from -3 to 3
- cross_output: bfloat16 [768, 768], P('tensor'), may hold values from -1.75 to 1.75
- cross_output_bias: float32 [768], replicated, may hold values from -2 to 2
- second_gain: float32 [768], replicated, may hold values from 0.25 to 1.75
- second_shift: float32 [768], replicated, may hold values from -2 to 2
- expand_weight: bfloat16 [768, 3072], P(None, 'tensor'), may hold values from -0.21875 to 0.21875
- expand_bias: float32 [3072], P('tensor'), may hold values from -3 to 3
- contract_weight: bfloat16 [3072, 768], P('tensor'), may hold values from -0.21875 to 0.21875
- contract_bias: float32 [768], replicated, may hold values from -2 to 2
- third_gain: float32 [768], replicated, may hold values from 0.25 to 1.75
- third_shift: float32 [768], replicated, may hold values from -2 to 2
- output_grad: bfloat16 [8192, 768], P('dp'), may hold values from -6 to 6
Outputs:
- layer_output: bfloat16 [8192, 768], P('dp')
- target_grad: bfloat16 [8192, 768], P('dp', 'tensor')
- memory_grad: bfloat16 [8192, 768], P('dp', 'tensor')
- grad_self_query: float32 [768, 768], P('dp', 'tensor')
- grad_self_query_bias: float32 [768], P('tensor')
- grad_self_key: float32 [768, 768], P('dp', 'tensor')
- grad_self_value: float32 [768, 768], P('dp', 'tensor')
- grad_self_value_bias: float32 [768], P('tensor')
- grad_self_output: float32 [768, 768], P('tensor', 'dp')
- grad_self_output_bias: float32 [768], replicated
- grad_first_gain: float32 [768], replicated
- grad_first_shift: float32 [768], replicated
- grad_cross_query: float32 [768, 768], P('dp', 'tensor')
- grad_cross_query_bias: float32 [768], P('tensor')
- grad_cross_key: float32 [768, 768], P('dp', 'tensor')
- grad_cross_value: float32 [768, 768], P('dp', 'tensor')
- grad_cross_value_bias: float32 [768], P('tensor')
- grad_cross_output: float32 [768, 768], P('tensor', 'dp')
- grad_cross_output_bias: float32 [768], replicated
- grad_second_gain: float32 [768], replicated
- grad_second_shift: float32 [768], replicated
- grad_expand_weight: float32 [768, 3072], P('dp', 'tensor')
- grad_expand_bias: float32 [3072], P('tensor')
- grad_contract_weight: float32 [3072, 768], P('tensor', 'dp')
- grad_contract_bias: float32 [768], replicated
- grad_third_gain: float32 [768], replicated
- grad_third_shift: float32 [768], replicated
Inputs may be any that keep to these rules, and one draw needn't show every extreme that they name: `target_segments`: along each row the ids never fall. Ids 0 to 3 are documents, every one present in every row with one or more positions; id 4 marks the padding at the row's end, 1 to 128 positions, and appears in every row. `memory_segments`: same law as target_segments, drawn independently: document d of a memory row belongs to document d of the same target row, and padding of target rows reads padding of memory rows.
All inputs are finite; a program needn't handle non-finite values.
Results may differ from a plain program's by a relative error of at most 0.025.
The roundings to bfloat16 on the way count: a program that leaves them out, or rounds other values in their place, can miss the bound.
Values sent between devices are 32-bit elements; how exact they have to be, the bound alone decides.
A program may use at most 128 MiB of HBM per device.

v0:
```python
from functools import partial
import jax
import jax.numpy as jnp
from jax import lax
from jax.sharding import PartitionSpec as P

HEAD_DIM = 64
EPSILON = 1e-05
NEGATIVE = -1e30


def normalize(summed, norm_gain, norm_shift):
    center = jnp.mean(summed, axis=-1, keepdims=True)
    centered = summed - center
    spread = jnp.mean(centered * centered, axis=-1, keepdims=True)
    return centered * lax.rsqrt(spread + EPSILON) * norm_gain + norm_shift


def exact_gelu(values):
    return jax.nn.gelu(values, approximate=False)


def matmul(left_side, right_side):
    return jnp.dot(left_side, right_side, preferred_element_type=jnp.float32)


def contract_rows(left_side, right_side):
    return lax.dot_general(
        left_side, right_side, (((0,), (0,)), ((), ())), preferred_element_type=jnp.float32
    )


def times_transpose(left_side, right_side):
    return lax.dot_general(
        left_side, right_side, (((1,), (1,)), ((), ())), preferred_element_type=jnp.float32
    )


def column_sums(values):
    return jnp.sum(values.astype(jnp.float32), axis=0)


def block_scores(chosen, key_rows, chosen_ids, key_ids, first_row, causal):
    block_rows = chosen.shape[0]
    allowed = chosen_ids[:, None] == key_ids[None, :]
    if causal:
        query_pos = first_row + jnp.arange(block_rows, dtype=jnp.int32)
        key_pos = jnp.arange(key_rows.shape[0], dtype=jnp.int32)
        allowed = allowed & (query_pos[:, None] >= key_pos[None, :])
    scores = jnp.einsum(
        "qhd,khd->hqk", chosen, key_rows, preferred_element_type=jnp.float32
    ) * chosen.shape[2] ** (-0.5)
    return jnp.where(allowed[None], scores, NEGATIVE)


def attend_row(causal, items):
    query_rows, key_rows, value_rows, query_ids, key_ids = items
    length = query_rows.shape[0]
    block_rows = min(512, length)

    def one_block(block_index):
        first_row = block_index * block_rows
        chosen = lax.dynamic_slice_in_dim(query_rows, first_row, block_rows, 0)
        chosen_ids = lax.dynamic_slice_in_dim(query_ids, first_row, block_rows, 0)
        scores = block_scores(chosen, key_rows, chosen_ids, key_ids, first_row, causal)
        row_max = jnp.max(scores, axis=-1, keepdims=True)
        exponent = jnp.exp(scores - row_max)
        row_sum = jnp.sum(exponent, axis=-1, keepdims=True)
        weights_low = (exponent / row_sum).astype(jnp.bfloat16)
        mixture = jnp.einsum(
            "hqk,khd->qhd", weights_low, value_rows, preferred_element_type=jnp.float32
        )
        return (mixture.astype(jnp.bfloat16), (row_max + jnp.log(row_sum))[..., 0])

    mixture, log_sums = lax.map(one_block, jnp.arange(length // block_rows, dtype=jnp.int32))
    return (mixture.reshape(query_rows.shape), log_sums)


def attend_back(causal, items):
    query_rows, key_rows, value_rows, query_ids, key_ids, log_sums, grad_mixture = items
    length = query_rows.shape[0]
    block_rows = min(512, length)
    score_scale = query_rows.shape[2] ** (-0.5)

    def one_block(carry, block_items):
        block_index, block_sums = block_items
        key_accum, value_accum = carry
        first_row = block_index * block_rows
        chosen = lax.dynamic_slice_in_dim(query_rows, first_row, block_rows, 0)
        chosen_ids = lax.dynamic_slice_in_dim(query_ids, first_row, block_rows, 0)
        chosen_grad = lax.dynamic_slice_in_dim(grad_mixture, first_row, block_rows, 0)
        scores = block_scores(chosen, key_rows, chosen_ids, key_ids, first_row, causal)
        weights_soft = jnp.exp(scores - block_sums[..., None])
        weights_low = weights_soft.astype(jnp.bfloat16)
        grad_weights = jnp.einsum(
            "qhd,khd->hqk", chosen_grad, value_rows, preferred_element_type=jnp.float32
        )
        row_dot = jnp.sum(weights_soft * grad_weights, axis=-1, keepdims=True)
        grad_scores = (weights_soft * (grad_weights - row_dot)).astype(jnp.bfloat16)
        grad_chosen = (
            jnp.einsum("hqk,khd->qhd", grad_scores, key_rows, preferred_element_type=jnp.float32)
            * score_scale
        )
        key_accum = (
            key_accum
            + jnp.einsum("hqk,qhd->khd", grad_scores, chosen, preferred_element_type=jnp.float32)
            * score_scale
        )
        value_accum = value_accum + jnp.einsum(
            "hqk,qhd->khd", weights_low, chosen_grad, preferred_element_type=jnp.float32
        )
        return ((key_accum, value_accum), grad_chosen.astype(jnp.bfloat16))

    zeros_start = jnp.zeros(key_rows.shape, jnp.float32)
    carried, grad_blocks = lax.scan(
        one_block,
        (zeros_start, zeros_start),
        (jnp.arange(length // block_rows, dtype=jnp.int32), log_sums),
    )
    return (
        grad_blocks.reshape(query_rows.shape),
        carried[0].astype(jnp.bfloat16),
        carried[1].astype(jnp.bfloat16),
    )


def per_device(
    target,
    memory,
    target_segments,
    memory_segments,
    self_query,
    self_query_bias,
    self_key,
    self_value,
    self_value_bias,
    self_output,
    self_output_bias,
    first_gain,
    first_shift,
    cross_query,
    cross_query_bias,
    cross_key,
    cross_value,
    cross_value_bias,
    cross_output,
    cross_output_bias,
    second_gain,
    second_shift,
    expand_weight,
    expand_bias,
    contract_weight,
    contract_bias,
    third_gain,
    third_shift,
    output_grad,
):
    row_count = target_segments.shape[0]
    local_width = self_query.shape[1]
    head_count = local_width // HEAD_DIM

    def to_heads(matrix):
        return matrix.reshape(row_count, -1, head_count, HEAD_DIM)

    def to_tokens(stacked):
        return stacked.reshape(-1, local_width)

    def branch_total(partial_term):
        return lax.psum(partial_term, "tensor")

    def input_total(partial_term):
        return lax.psum(partial_term, "tensor")

    def edge_total(partial_term):
        return lax.psum_scatter(partial_term, "tensor", scatter_dimension=1, tiled=True)

    self_queries = (matmul(target, self_query) + self_query_bias).astype(jnp.bfloat16)
    self_keys = matmul(target, self_key).astype(jnp.bfloat16)
    self_values = (matmul(target, self_value) + self_value_bias).astype(jnp.bfloat16)
    self_mixture, self_sums = lax.map(
        partial(attend_row, True),
        (
            to_heads(self_queries),
            to_heads(self_keys),
            to_heads(self_values),
            target_segments,
            target_segments,
        ),
    )
    self_mixed = to_tokens(self_mixture)
    self_branch = branch_total(matmul(self_mixed, self_output)) + self_output_bias
    first_norm, first_back = jax.vjp(
        normalize, target.astype(jnp.float32) + self_branch, first_gain, first_shift
    )
    first_low = first_norm.astype(jnp.bfloat16)
    cross_queries = (matmul(first_low, cross_query) + cross_query_bias).astype(jnp.bfloat16)
    cross_keys = matmul(memory, cross_key).astype(jnp.bfloat16)
    cross_values = (matmul(memory, cross_value) + cross_value_bias).astype(jnp.bfloat16)
    cross_mixture, cross_sums = lax.map(
        partial(attend_row, False),
        (
            to_heads(cross_queries),
            to_heads(cross_keys),
            to_heads(cross_values),
            target_segments,
            memory_segments,
        ),
    )
    cross_mixed = to_tokens(cross_mixture)
    cross_branch = branch_total(matmul(cross_mixed, cross_output)) + cross_output_bias
    second_norm, second_back = jax.vjp(
        normalize, first_norm + cross_branch, second_gain, second_shift
    )
    second_low = second_norm.astype(jnp.bfloat16)
    hidden = matmul(second_low, expand_weight) + expand_bias
    activated_float, gelu_back = jax.vjp(exact_gelu, hidden)
    activated = activated_float.astype(jnp.bfloat16)
    ffn_branch = branch_total(matmul(activated, contract_weight)) + contract_bias
    final_norm, third_back = jax.vjp(normalize, second_norm + ffn_branch, third_gain, third_shift)
    layer_output = final_norm.astype(jnp.bfloat16)
    grad_third_sum, grad_third_gain, grad_third_shift = third_back(output_grad.astype(jnp.float32))
    grad_ffn = grad_third_sum.astype(jnp.bfloat16)
    grad_contract_weight = contract_rows(activated, grad_ffn)
    grad_contract_bias = column_sums(grad_ffn)
    grad_hidden = gelu_back(times_transpose(grad_ffn, contract_weight))[0].astype(jnp.bfloat16)
    grad_expand_weight = contract_rows(second_low, grad_hidden)
    grad_expand_bias = column_sums(grad_hidden)
    ffn_summed = (grad_expand_weight, grad_contract_weight)
    grad_second = grad_third_sum + input_total(times_transpose(grad_hidden, expand_weight))
    grad_second_sum, grad_second_gain, grad_second_shift = second_back(grad_second)
    grad_cross = grad_second_sum.astype(jnp.bfloat16)
    grad_cross_output = contract_rows(cross_mixed, grad_cross)
    grad_cross_output_bias = column_sums(grad_cross)
    grad_cross_mixed = times_transpose(grad_cross, cross_output).astype(jnp.bfloat16)
    cross_grads = lax.map(
        partial(attend_back, False),
        (
            to_heads(cross_queries),
            to_heads(cross_keys),
            to_heads(cross_values),
            target_segments,
            memory_segments,
            cross_sums,
            to_heads(grad_cross_mixed),
        ),
    )
    grad_cross_queries = to_tokens(cross_grads[0])
    grad_cross_keys = to_tokens(cross_grads[1])
    grad_cross_values = to_tokens(cross_grads[2])
    grad_cross_query = contract_rows(first_low, grad_cross_queries)
    grad_cross_query_bias = column_sums(grad_cross_queries)
    grad_cross_key = contract_rows(memory, grad_cross_keys)
    grad_cross_value = contract_rows(memory, grad_cross_values)
    grad_cross_value_bias = column_sums(grad_cross_values)
    cross_summed = (grad_cross_query, grad_cross_key, grad_cross_value, grad_cross_output)
    memory_share = edge_total(
        times_transpose(grad_cross_keys, cross_key)
        + times_transpose(grad_cross_values, cross_value)
    )
    memory_grad = memory_share.astype(jnp.bfloat16)
    grad_first = grad_second_sum + input_total(times_transpose(grad_cross_queries, cross_query))
    grad_first_sum, grad_first_gain, grad_first_shift = first_back(grad_first)
    grad_self = grad_first_sum.astype(jnp.bfloat16)
    grad_self_output = contract_rows(self_mixed, grad_self)
    grad_self_output_bias = column_sums(grad_self)
    grad_self_mixed = times_transpose(grad_self, self_output).astype(jnp.bfloat16)
    self_grads = lax.map(
        partial(attend_back, True),
        (
            to_heads(self_queries),
            to_heads(self_keys),
            to_heads(self_values),
            target_segments,
            target_segments,
            self_sums,
            to_heads(grad_self_mixed),
        ),
    )
    grad_self_queries = to_tokens(self_grads[0])
    grad_self_keys = to_tokens(self_grads[1])
    grad_self_values = to_tokens(self_grads[2])
    grad_self_query = contract_rows(target, grad_self_queries)
    grad_self_query_bias = column_sums(grad_self_queries)
    grad_self_key = contract_rows(target, grad_self_keys)
    grad_self_value = contract_rows(target, grad_self_values)
    grad_self_value_bias = column_sums(grad_self_values)
    self_summed = (grad_self_query, grad_self_key, grad_self_value, grad_self_output)
    target_term = (
        times_transpose(grad_self_queries, self_query)
        + times_transpose(grad_self_keys, self_key)
        + times_transpose(grad_self_values, self_value)
    )
    target_share = edge_total(target_term)
    share_width = target_share.shape[1]
    residual_part = lax.dynamic_slice_in_dim(
        grad_first_sum, lax.axis_index("tensor") * share_width, share_width, 1
    )
    target_grad = (target_share + residual_part).astype(jnp.bfloat16)
    summed = (
        lax.psum_scatter(self_summed[0], "dp", scatter_dimension=0, tiled=True),
        lax.psum_scatter(self_summed[1], "dp", scatter_dimension=0, tiled=True),
        lax.psum_scatter(self_summed[2], "dp", scatter_dimension=0, tiled=True),
        lax.psum_scatter(self_summed[3], "dp", scatter_dimension=1, tiled=True),
        lax.psum_scatter(cross_summed[0], "dp", scatter_dimension=0, tiled=True),
        lax.psum_scatter(cross_summed[1], "dp", scatter_dimension=0, tiled=True),
        lax.psum_scatter(cross_summed[2], "dp", scatter_dimension=0, tiled=True),
        lax.psum_scatter(cross_summed[3], "dp", scatter_dimension=1, tiled=True),
        lax.psum_scatter(ffn_summed[0], "dp", scatter_dimension=0, tiled=True),
        lax.psum_scatter(ffn_summed[1], "dp", scatter_dimension=1, tiled=True),
    )
    vectors = lax.psum(
        (
            grad_self_query_bias,
            grad_self_value_bias,
            grad_self_output_bias,
            grad_first_gain,
            grad_first_shift,
            grad_cross_query_bias,
            grad_cross_value_bias,
            grad_cross_output_bias,
            grad_second_gain,
            grad_second_shift,
            grad_expand_bias,
            grad_contract_bias,
            grad_third_gain,
            grad_third_shift,
        ),
        "dp",
    )
    return (
        layer_output,
        target_grad,
        memory_grad,
        summed[0],
        vectors[0],
        summed[1],
        summed[2],
        vectors[1],
        summed[3],
        vectors[2],
        vectors[3],
        vectors[4],
        summed[4],
        vectors[5],
        summed[5],
        summed[6],
        vectors[6],
        summed[7],
        vectors[7],
        vectors[8],
        vectors[9],
        summed[8],
        vectors[10],
        summed[9],
        vectors[11],
        vectors[12],
        vectors[13],
    )


def solution(mesh):
    in_specs = (
        P("dp", None),
        P("dp", None),
        P("dp", None),
        P("dp", None),
        P(None, "tensor"),
        P("tensor"),
        P(None, "tensor"),
        P(None, "tensor"),
        P("tensor"),
        P("tensor", None),
        P(),
        P(),
        P(),
        P(None, "tensor"),
        P("tensor"),
        P(None, "tensor"),
        P(None, "tensor"),
        P("tensor"),
        P("tensor", None),
        P(),
        P(),
        P(),
        P(None, "tensor"),
        P("tensor"),
        P("tensor", None),
        P(),
        P(),
        P(),
        P("dp", None),
    )
    out_specs = (
        P("dp", None),
        P("dp", "tensor"),
        P("dp", "tensor"),
        P("dp", "tensor"),
        P("tensor"),
        P("dp", "tensor"),
        P("dp", "tensor"),
        P("tensor"),
        P("tensor", "dp"),
        P(),
        P(),
        P(),
        P("dp", "tensor"),
        P("tensor"),
        P("dp", "tensor"),
        P("dp", "tensor"),
        P("tensor"),
        P("tensor", "dp"),
        P(),
        P(),
        P(),
        P("dp", "tensor"),
        P("tensor"),
        P("tensor", "dp"),
        P(),
        P(),
        P(),
    )
    return jax.shard_map(
        per_device, mesh=mesh, in_specs=in_specs, out_specs=out_specs, check_vma=False
    )
```

profile of v0, /device:TPU:0, one launch (start us, length us, event | category | flops | bytes accessed | tf_op | source)
XLA Modules:
  0.0 1282.4 jit_solution(13164069724947715396)
XLA Ops:
  15.3 19.3 %while.96 = (s32[]{:T(128)}, bf16[2,512,3,64]{1,3,2,0:T(8,128)(2,1)}, f32[2,3,512]{2,1,0:T(4,128)}, s32[2]{0:T(128)S(1)}, s32[1024]{0:T(1024)S(1)}, /*index=5*/b...) while((s32[]{:T(128)}, ...), condition=%wide.region_3.4_spmd, body=%wide.region_0.3_spmd.sunk | while | flops 423197696 | bytes 27042136 | solution.py:75
  44.6 119.6 %all-reduce.7.cloned.1.call-done = f32[1024,768]{1,0:T(8,128)} async-done(((f32[1024,768]{1,0:T(8,128)}), f32[1024,768]{1,0:T(8,128)}) %all-reduce.7.cloned.1.call-update) | async-done | bytes 3145744 | tf_op jit(solution)/shard_map/psum | solution.py:169
  170.4 14.2 %while.97 = (s32[]{:T(128)}, bf16[2,512,3,64]{1,3,2,0:T(8,128)(2,1)S(1)}, f32[2,3,512]{2,1,0:T(4,128)S(1)}, s32[2]{0:T(128)S(1)}, s32[1024]{0:T(1024)S(1)}, /*in...) while((s32[]{:T(128)}, ...), condition=%wide.region_10.11_spmd, body=%wide.region_7.10_spmd.sunk | while | flops 422148608 | bytes 22221008 | solution.py:75
  190.3 119.8 %all-reduce.9.cloned.1.call-done = f32[1024,768]{1,0:T(8,128)} async-done(((f32[1024,768]{1,0:T(8,128)}), f32[1024,768]{1,0:T(8,128)}) %all-reduce.9.cloned.1.call-update) | async-done | bytes 3145744 | tf_op jit(solution)/shard_map/psum | solution.py:169
  316.2 9.8 multiply_convert_fusion.2
  330.3 120.2 %all-reduce.11.cloned.1.call-done = f32[1024,768]{1,0:T(8,128)} async-done(((f32[1024,768]{1,0:T(8,128)}), f32[1024,768]{1,0:T(8,128)}) %all-reduce.11.cloned.1.call-update) | async-done | bytes 3145744 | tf_op jit(solution)/shard_map/psum | solution.py:169
  471.0 120.0 %all-reduce.13.cloned.1.call-done = f32[1024,768]{1,0:T(8,128)} async-done(((f32[1024,768]{1,0:T(8,128)}), f32[1024,768]{1,0:T(8,128)}) %all-reduce.13.cloned.1.call-update) | async-done | bytes 3145744 | tf_op jit(solution)/shard_map/psum | solution.py:172
  591.0 5.4 multiply_reduce_fusion.2
  601.3 23.7 %while.98 = (s32[]{:T(128)}, f32[1024,3,64]{0,2,1:T(8,128)S(1)}, f32[1024,3,64]{0,2,1:T(8,128)}, bf16[2,512,3,64]{1,3,2,0:T(8,128)(2,1)}, s32[2]{0:T(128)S(1)}, ...) while((s32[]{:T(128)}, f32[1024,3,64]{0,2,1:T(8,128)S(1)}, ...), condition=%wide.region_24.25_spmd.clone, body=%wide.region_22.24_spmd.clone.sunk | while | flops 1031928320 | bytes 65659268 | solution.py:115
  634.3 115.9 %all-reduce.15.cloned.1.call-done = f32[1024,768]{1,0:T(8,128)} async-done(((f32[1024,768]{1,0:T(8,128)}), f32[1024,768]{1,0:T(8,128)}) %all-reduce.15.cloned.1.call-update) | async-done | bytes 3145744 | tf_op jit(solution)/shard_map/psum | solution.py:172
  750.2 5.4 multiply_reduce_fusion.3
  771.5 24.3 %while.99 = (s32[]{:T(128)}, f32[1024,3,64]{0,2,1:T(8,128)S(1)}, f32[1024,3,64]{0,2,1:T(8,128)}, bf16[2,512,3,64]{1,3,2,0:T(8,128)(2,1)}, s32[2]{0:T(128)S(1)}, ...) while((s32[]{:T(128)}, f32[1024,3,64]{0,2,1:T(8,128)S(1)}, ...), condition=%wide.region_30.31_spmd.clone, body=%wide.region_28.30_spmd.clone.sunk | while | flops 1032977408 | bytes 65663364 | solution.py:115
  807.7 5.6 fusion.106
  842.3 25.8 %all-reduce = (f32[192]{0:T(256)}, f32[192]{0:T(256)}, f32[768]{0:T(1024)}, f32[768]{0:T(1024)}, f32[768]{0:T(1024)}, /*index=5*/f32[192]{0:T(256)}, f32[192]{0:...) all-reduce(f32[192]{0:T(256)S(1)} %reduce_sum.341, ...), channel_id=1, replica_groups=mesh['dp'=8,'tensor'=4] {'dp'}, use_global_device_ids=true, to_apply=%region_35.36 | all-reduce | flops 8448 | bytes 67584 | tf_op jit(solution)/shard_map/psum | solution.py:311
  869.7 18.2 %reduce-scatter.29.cloned.1.call-done = f32[1024,192]{0,1:T(8,128)} async-done(((f32[1024,768]{0,1:T(8,128)}), f32[1024,192]{0,1:T(8,128)}) %reduce-scatter.29.cloned.1.call-update) | async-done | bytes 786448 | tf_op jit(solution)/shard_map/reduce_scatter | solution.py:175
  889.9 60.7 %reduce-scatter.37.cloned.1.call-done = f32[192,1024]{1,0:T(8,128)} async-done(((f32[768,1024]{1,0:T(8,128)}), f32[192,1024]{1,0:T(8,128)}) %reduce-scatter.37.cloned.1.call-update) | async-done | bytes 786448
  954.8 42.2 %reduce-scatter.35.cloned.1.call-done = f32[768,96]{0,1:T(8,128)} async-done(((f32[768,768]{0,1:T(8,128)}), f32[768,96]{0,1:T(8,128)}) %reduce-scatter.35.cloned.1.call-update) | async-done | bytes 294928 | tf_op jit(solution)/shard_map/reduce_scatter | solution.py:309
  996.9 46.8 %reduce-scatter.33.cloned.1.call-done = f32[96,768]{1,0:T(8,128)} async-done(((f32[768,768]{1,0:T(8,128)}), f32[96,768]{1,0:T(8,128)}) %reduce-scatter.33.cloned.1.call-update) | async-done | bytes 294928 | tf_op jit(solution)/shard_map/reduce_scatter | solution.py:308
  1043.7 38.6 %reduce-scatter.31.cloned.1.call-done = f32[96,192]{1,0:T(8,128)} async-done(((f32[768,192]{1,0:T(8,128)}), f32[96,192]{1,0:T(8,128)}) %reduce-scatter.31.cloned.1.call-update) | async-done | bytes 73744 | tf_op jit(solution)/shard_map/reduce_scatter | solution.py:304
  1082.3 38.7 %reduce-scatter.49.cloned.1.call-done = f32[96,192]{1,0:T(8,128)} async-done(((f32[768,192]{1,0:T(8,128)}), f32[96,192]{1,0:T(8,128)}) %reduce-scatter.49.cloned.1.call-update) | async-done | bytes 73744
  1121.1 38.6 %reduce-scatter.47.cloned.1.call-done = f32[96,192]{1,0:T(8,128)} async-done(((f32[768,192]{1,0:T(8,128)}), f32[96,192]{1,0:T(8,128)}) %reduce-scatter.47.cloned.1.call-update) | async-done | bytes 73744
  1159.7 38.6 %reduce-scatter.43.cloned.1.call-done = f32[96,192]{1,0:T(8,128)} async-done(((f32[768,192]{1,0:T(8,128)}), f32[96,192]{1,0:T(8,128)}) %reduce-scatter.43.cloned.1.call-update) | async-done | bytes 73744
  1198.3 38.6 %reduce-scatter.39.cloned.1.call-done = f32[96,192]{1,0:T(8,128)} async-done(((f32[768,192]{1,0:T(8,128)}), f32[96,192]{1,0:T(8,128)}) %reduce-scatter.39.cloned.1.call-update) | async-done | bytes 73744
  1236.9 38.6 %reduce-scatter.41.cloned.1.call-done = f32[96,192]{1,0:T(8,128)} async-done(((f32[768,192]{1,0:T(8,128)}), f32[96,192]{1,0:T(8,128)}) %reduce-scatter.41.cloned.1.call-update) | async-done | bytes 73744
  (451 shorter events, 213.9 us)
Async XLA Ops:
  7.2 157.0 %all-reduce.7.cloned.1.call-start = ((), (), s32[]{:S(2)}) async-start(), calls=%async_computation.12 | async-start | bytes 6291456 | tf_op jit(solution)/shard_map/psum | solution.py:169
  40.3 123.9 %copy-start.89 = (f32[768]{0:T(1024)S(1)}, f32[768]{0:T(1024)}, u32[]{:S(2)}) copy-start(f32[768]{0:T(1024)} %param.47) | copy-start | bytes 9220
  40.3 269.7 %all-reduce.9.cloned.1.call-start = ((), (), s32[]{:S(2)}) async-start(), calls=%async_computation.13 | async-start | bytes 6291456 | tf_op jit(solution)/shard_map/psum | solution.py:169
  168.2 141.9 %copy-start.58 = (f32[1024]{0:T(1024)}, f32[1024]{0:T(1024)S(1)}, u32[]{:S(2)}) copy-start(f32[1024]{0:T(1024)S(1)} %fusion.94) | copy-start | bytes 12292
  186.4 123.6 %copy-start.61 = (f32[768]{0:T(1024)S(1)}, f32[768]{0:T(1024)}, u32[]{:S(2)}) copy-start(f32[768]{0:T(1024)} %param.48) | copy-start | bytes 9220
  186.4 123.6 %copy-start.81 = (f32[768]{0:T(1024)S(1)}, f32[768]{0:T(1024)}, u32[]{:S(2)}) copy-start(f32[768]{0:T(1024)} %param.49) | copy-start | bytes 9220
  186.4 123.6 %copy-start.90 = (f32[768]{0:T(1024)S(1)}, f32[768]{0:T(1024)}, u32[]{:S(2)}) copy-start(f32[768]{0:T(1024)} %param.56) | copy-start | bytes 9220
  189.8 260.7 %all-reduce.11.cloned.1.call-start = ((), (), s32[]{:S(2)}) async-start(), calls=%async_computation.14 | async-start | bytes 6291456 | tf_op jit(solution)/shard_map/psum | solution.py:169
  314.0 282.4 %copy-start.56 = (f32[1024]{0:T(1024)}, f32[1024]{0:T(1024)S(1)}, u32[]{:S(2)}) copy-start(f32[1024]{0:T(1024)S(1)} %broadcast_multiply_fusion.1) | copy-start | bytes 12292
  316.2 134.3 %copy-start.63 = (f32[1024]{0:T(1024)}, f32[1024]{0:T(1024)S(1)}, u32[]{:S(2)}) copy-start(f32[1024]{0:T(1024)S(1)} %fusion.95) | copy-start | bytes 12292
  330.3 260.7 %all-reduce.13.cloned.1.call-start = ((), (), s32[]{:S(2)}) async-start(), calls=%async_computation.15 | async-start | bytes 6291456 | tf_op jit(solution)/shard_map/psum | solution.py:172
  470.7 279.5 %all-reduce.15.cloned.1.call-start = ((), (), s32[]{:S(2)}) async-start(), calls=%async_computation.16 | async-start | bytes 6291456 | tf_op jit(solution)/shard_map/psum | solution.py:172
  630.0 209.3 %reduce-scatter.51.cloned.1.call-start = ((), (), s32[]{:S(2)}) async-start(), calls=%async_computation.28 | async-start | bytes 884736
  634.0 234.1 %reduce-scatter.45.cloned.1.call-start = ((), (), s32[]{:S(2)}) async-start(), calls=%async_computation.25 | async-start | bytes 884736
  761.3 126.6 %reduce-scatter.29.cloned.1.call-start = ((), (), s32[]{:S(2)}) async-start(), calls=%async_computation.17 | async-start | bytes 3932160 | tf_op jit(solution)/shard_map/reduce_scatter | solution.py:175
  767.3 183.3 %reduce-scatter.37.cloned.1.call-start = ((), (), s32[]{:S(2)}) async-start(), calls=%async_computation.21 | async-start | bytes 3932160
  802.0 195.0 %reduce-scatter.35.cloned.1.call-start = ((), (), s32[]{:S(2)}) async-start(), calls=%async_computation.20 | async-start | bytes 2654208 | tf_op jit(solution)/shard_map/reduce_scatter | solution.py:309
  807.6 236.2 %reduce-scatter.33.cloned.1.call-start = ((), (), s32[]{:S(2)}) async-start(), calls=%async_computation.19 | async-start | bytes 2654208 | tf_op jit(solution)/shard_map/reduce_scatter | solution.py:308
  813.3 269.0 %reduce-scatter.31.cloned.1.call-start = ((), (), s32[]{:S(2)}) async-start(), calls=%async_computation.18 | async-start | bytes 884736 | tf_op jit(solution)/shard_map/reduce_scatter | solution.py:304
  815.9 305.2 %reduce-scatter.49.cloned.1.call-start = ((), (), s32[]{:S(2)}) async-start(), calls=%async_computation.27 | async-start | bytes 884736
  820.6 339.0 %reduce-scatter.47.cloned.1.call-start = ((), (), s32[]{:S(2)}) async-start(), calls=%async_computation.26 | async-start | bytes 884736
  825.3 373.0 %reduce-scatter.43.cloned.1.call-start = ((), (), s32[]{:S(2)}) async-start(), calls=%async_computation.24 | async-start | bytes 884736
  828.9 407.9 %reduce-scatter.39.cloned.1.call-start = ((), (), s32[]{:S(2)}) async-start(), calls=%async_computation.22 | async-start | bytes 884736
  833.5 441.9 %reduce-scatter.41.cloned.1.call-start = ((), (), s32[]{:S(2)}) async-start(), calls=%async_computation.23 | async-start | bytes 884736
  (116 other events, 1006.3 us)
Sparse Core Ops, SparseCore 0:
  40.4 123.7 all-reduce.6
  189.9 120.0 all-reduce.8
  330.4 120.0 all-reduce.10
  470.8 120.0 all-reduce.12
  630.0 120.0 all-reduce.14
  753.2 33.9 reduce-scatter.50
  790.3 34.9 reduce-scatter.44
  827.7 60.2 reduce-scatter.28
  890.3 60.2 reduce-scatter.36
  954.4 42.5 reduce-scatter.34
  1001.2 42.4 reduce-scatter.32
  1047.3 34.9 reduce-scatter.30
  1086.0 34.9 reduce-scatter.48
  1124.6 34.9 reduce-scatter.46
  1163.2 34.9 reduce-scatter.42
  1201.8 34.9 reduce-scatter.38
  1240.4 34.9 reduce-scatter.40
where the time goes:
time: 1290 us; the launch traced here: 1280 us
  waiting for transfers between devices  995 us (77%)
  matrix products  125 us (10%)
  other arithmetic  60.8 us (5%)
  local copies, waits for them, and re-layouts  52.4 us (4%)
  blocking collectives  25.8 us (2%)
  between operations  15.5 us (1%)
    psum x3, waiting for transfers between devices, branch_total(): return lax.psum(partial_term, 'tensor')  360 us
    unnamed x25, waiting for transfers between devices  254 us
    psum x2, waiting for transfers between devices, input_total(): return lax.psum(partial_term, 'tensor')  236 us
    reduce_scatter x1, waiting for transfers between devices, per_device(): lax.psum_scatter(ffn_summed[0], 'dp', scatter_dimension=0, tiled=True)  46.8 us
    reduce_scatter x1, waiting for transfers between devices, per_device(): lax.psum_scatter(ffn_summed[1], 'dp', scatter_dimension=1, tiled=True)  42.2 us
    reduce_scatter x1, waiting for transfers between devices, per_device(): lax.psum_scatter(cross_summed[0], 'dp', scatter_dimension=0, tiled=True)  38.6 us
    unnamed x199, local copies, waits for them, and re-layouts  31.8 us
    dot_general x10, matrix products, matmul(): return jnp.dot(left_side, right_side, preferred_element_type=jnp.float32)  30.7 us
  transfers between devices with their start and end apart: 17, of which 15 were waited for; matrix products, arithmetic and copies ran while one was open for 8% of the time, Pallas kernels for 0%

commit v1 on v0

--- a/solution.py
+++ b/solution.py
@@ -169,7 +169,7 @@
         return lax.psum(partial_term, "tensor")
 
     def input_total(partial_term):
-        return lax.psum(partial_term, "tensor")
+        return jnp.sum(lax.all_gather(partial_term, "tensor"), axis=0)
 
     def edge_total(partial_term):
         return lax.psum_scatter(partial_term, "tensor", scatter_dimension=1, tiled=True)

time: 1290 us -> 1490 us (1.16)
  waiting for transfers between devices: 995 us -> 1180 us
    all_gather x0 -> x2, waiting for transfers between devices: none -> 425 us  [input_total(): return jnp.sum(lax.all_gather(partial_term, 'tensor'), axis=0)]
    psum x2 -> x0, waiting for transfers between devices: 236 us -> none  [input_total(): return lax.psum(partial_term, 'tensor')]
    reduce_sum x0 -> x2, other arithmetic: none -> 14.9 us  [input_total(): return jnp.sum(lax.all_gather(partial_term, 'tensor'), axis=0)]
    unnamed x199 -> x205, local copies, waits for them, and re-layouts: 31.8 us -> 33.1 us
  transfers between devices with their start and end apart: 17 -> 17, of which waited for: 15 -> 16; matrix products, arithmetic and copies ran while one was open for 8% -> 7% of each run, Pallas kernels for 0% -> 0%
where the time goes in v1:
time: 1490 us; the launch traced here: 1480 us
  waiting for transfers between devices  1180 us (79%)
  matrix products  127 us (9%)
  other arithmetic  73.4 us (5%)
  local copies, waits for them, and re-layouts  54.4 us (4%)
  blocking collectives  25 us (2%)
  between operations  15.3 us (1%)
    all_gather x2, waiting for transfers between devices, input_total(): return jnp.sum(lax.all_gather(partial_term, 'tensor'), axis=0)  425 us
    psum x3, waiting for transfers between devices, branch_total(): return lax.psum(partial_term, 'tensor')  360 us
    unnamed x25, waiting for transfers between devices  265 us
    reduce_scatter x1, waiting for transfers between devices, per_device(): lax.psum_scatter(ffn_summed[0], 'dp', scatter_dimension=0, tiled=True)  46.8 us
    reduce_scatter x1, waiting for transfers between devices, per_device(): lax.psum_scatter(ffn_summed[1], 'dp', scatter_dimension=1, tiled=True)  42.1 us
    reduce_scatter x1, waiting for transfers between devices, per_device(): lax.psum_scatter(cross_summed[0], 'dp', scatter_dimension=0, tiled=True)  38.6 us
    unnamed x205, local copies, waits for them, and re-layouts  33.1 us
    dot_general x10, matrix products, matmul(): return jnp.dot(left_side, right_side, preferred_element_type=jnp.float32)  30.7 us
  transfers between devices with their start and end apart: 17, of which 16 were waited for; matrix products, arithmetic and copies ran while one was open for 7% of the time, Pallas kernels for 0%

profile of v1, /device:TPU:0, one launch (start us, length us, event | category | flops | bytes accessed | tf_op | source)
XLA Modules:
  0.0 1484.1 jit_solution(11295316932334717814)
XLA Ops:
  15.3 19.3 %while.96 = (s32[]{:T(128)}, bf16[2,512,3,64]{1,3,2,0:T(8,128)(2,1)}, f32[2,3,512]{2,1,0:T(4,128)}, s32[2]{0:T(128)S(1)}, s32[1024]{0:T(1024)S(1)}, /*index=5*/b...) while((s32[]{:T(128)}, ...), condition=%wide.region_3.4_spmd, body=%wide.region_0.3_spmd.sunk | while | flops 423197696 | bytes 27042136 | solution.py:75
  44.9 119.4 %all-reduce.5.cloned.1.call-done = f32[1024,768]{1,0:T(8,128)} async-done(((f32[1024,768]{1,0:T(8,128)}), f32[1024,768]{1,0:T(8,128)}) %all-reduce.5.cloned.1.call-update) | async-done | bytes 3145744 | tf_op jit(solution)/shard_map/psum | solution.py:169
  170.4 14.2 while.97
  190.0 120.0 %all-reduce.7.cloned.1.call-done = f32[1024,768]{1,0:T(8,128)} async-done(((f32[1024,768]{1,0:T(8,128)}), f32[1024,768]{1,0:T(8,128)}) %all-reduce.7.cloned.1.call-update) | async-done | bytes 3145744 | tf_op jit(solution)/shard_map/psum | solution.py:169
  316.1 9.8 multiply_convert_fusion.2
  330.3 120.2 %all-reduce.9.cloned.1.call-done = f32[1024,768]{1,0:T(8,128)} async-done(((f32[1024,768]{1,0:T(8,128)}), f32[1024,768]{1,0:T(8,128)}) %all-reduce.9.cloned.1.call-update) | async-done | bytes 3145744 | tf_op jit(solution)/shard_map/psum | solution.py:169
  471.1 216.9 %all-gather.5.cloned.1.call-done = f32[4096,768]{1,0:T(8,128)} async-done(((f32[1024,768]{1,0:T(8,128)}), f32[4096,768]{1,0:T(8,128)}) %all-gather.5.cloned.1.call-update) | async-done | bytes 12582928 | tf_op jit(solution)/shard_map/all_gather | solution.py:172
  688.0 7.5 reduce_sum.354
  706.4 25.0 %while.98 = (s32[]{:T(128)}, f32[1024,3,64]{0,2,1:T(8,128)S(1)}, f32[1024,3,64]{0,2,1:T(8,128)}, bf16[2,512,3,64]{1,3,2,0:T(8,128)(2,1)}, s32[2]{0:T(128)}, /*in...) while((s32[]{:T(128)}, f32[1024,3,64]{0,2,1:T(8,128)S(1)}, ...), condition=%wide.region_24.25_spmd.clone, body=%wide.region_22.24_spmd.clone.sunk | while | flops 1031928320 | bytes 65659268 | solution.py:115
  745.0 207.9 %all-gather.7.cloned.1.call-done = f32[4096,768]{1,0:T(8,128)} async-done(((f32[1024,768]{1,0:T(8,128)}), f32[4096,768]{1,0:T(8,128)}) %all-gather.7.cloned.1.call-update) | async-done | bytes 12582928 | tf_op jit(solution)/shard_map/all_gather | solution.py:172
  952.9 7.4 reduce_sum.357
  972.3 24.2 %while.99 = (s32[]{:T(128)}, f32[1024,3,64]{0,2,1:T(8,128)S(1)}, f32[1024,3,64]{0,2,1:T(8,128)}, bf16[2,512,3,64]{1,3,2,0:T(8,128)(2,1)}, s32[2]{0:T(128)S(1)}, ...) while((s32[]{:T(128)}, f32[1024,3,64]{0,2,1:T(8,128)S(1)}, ...), condition=%wide.region_30.31_spmd.clone, body=%wide.region_28.30_spmd.clone.sunk | while | flops 1032977408 | bytes 65663364 | solution.py:115
  1014.2 5.6 fusion.106
  1054.1 25.0 %all-reduce = (f32[192]{0:T(256)}, f32[192]{0:T(256)}, f32[768]{0:T(1024)}, f32[768]{0:T(1024)}, f32[768]{0:T(1024)}, /*index=5*/f32[192]{0:T(256)}, f32[192]{0:...) all-reduce(f32[192]{0:T(256)S(1)} %reduce_sum.361, ...), channel_id=1, replica_groups=mesh['dp'=8,'tensor'=4] {'dp'}, use_global_device_ids=true, to_apply=%region_35.36 | all-reduce | flops 8448 | bytes 67584 | tf_op jit(solution)/shard_map/psum | solution.py:311
  1079.0 10.9 reduce-scatter.45.cloned.1.call-done
  1091.6 61.0 %reduce-scatter.37.cloned.1.call-done = f32[192,1024]{1,0:T(8,128)} async-done(((f32[768,1024]{1,0:T(8,128)}), f32[192,1024]{1,0:T(8,128)}) %reduce-scatter.37.cloned.1.call-update) | async-done | bytes 786448
  1156.7 42.1 %reduce-scatter.35.cloned.1.call-done = f32[768,96]{0,1:T(8,128)} async-done(((f32[768,768]{0,1:T(8,128)}), f32[768,96]{0,1:T(8,128)}) %reduce-scatter.35.cloned.1.call-update) | async-done | bytes 294928 | tf_op jit(solution)/shard_map/reduce_scatter | solution.py:309
  1198.8 46.8 %reduce-scatter.33.cloned.1.call-done = f32[96,768]{1,0:T(8,128)} async-done(((f32[768,768]{1,0:T(8,128)}), f32[96,768]{1,0:T(8,128)}) %reduce-scatter.33.cloned.1.call-update) | async-done | bytes 294928 | tf_op jit(solution)/shard_map/reduce_scatter | solution.py:308
  1245.6 38.6 %reduce-scatter.31.cloned.1.call-done = f32[96,192]{1,0:T(8,128)} async-done(((f32[768,192]{1,0:T(8,128)}), f32[96,192]{1,0:T(8,128)}) %reduce-scatter.31.cloned.1.call-update) | async-done | bytes 73744 | tf_op jit(solution)/shard_map/reduce_scatter | solution.py:304
  1284.2 38.7 %reduce-scatter.49.cloned.1.call-done = f32[96,192]{1,0:T(8,128)} async-done(((f32[768,192]{1,0:T(8,128)}), f32[96,192]{1,0:T(8,128)}) %reduce-scatter.49.cloned.1.call-update) | async-done | bytes 73744
  1323.0 38.6 %reduce-scatter.47.cloned.1.call-done = f32[96,192]{1,0:T(8,128)} async-done(((f32[768,192]{1,0:T(8,128)}), f32[96,192]{1,0:T(8,128)}) %reduce-scatter.47.cloned.1.call-update) | async-done | bytes 73744
  1361.6 38.6 %reduce-scatter.43.cloned.1.call-done = f32[96,192]{1,0:T(8,128)} async-done(((f32[768,192]{1,0:T(8,128)}), f32[96,192]{1,0:T(8,128)}) %reduce-scatter.43.cloned.1.call-update) | async-done | bytes 73744
  1400.2 38.6 %reduce-scatter.39.cloned.1.call-done = f32[96,192]{1,0:T(8,128)} async-done(((f32[768,192]{1,0:T(8,128)}), f32[96,192]{1,0:T(8,128)}) %reduce-scatter.39.cloned.1.call-update) | async-done | bytes 73744
  1438.8 38.6 %reduce-scatter.41.cloned.1.call-done = f32[96,192]{1,0:T(8,128)} async-done(((f32[768,192]{1,0:T(8,128)}), f32[96,192]{1,0:T(8,128)}) %reduce-scatter.41.cloned.1.call-update) | async-done | bytes 73744
  (459 shorter events, 230.6 us)
Async XLA Ops:
  7.2 157.0 %all-reduce.5.cloned.1.call-start = ((), (), s32[]{:S(2)}) async-start(), calls=%async_computation.12 | async-start | bytes 6291456 | tf_op jit(solution)/shard_map/psum | solution.py:169
  40.3 123.9 %copy-start.92 = (f32[768]{0:T(1024)S(1)}, f32[768]{0:T(1024)}, u32[]{:S(2)}) copy-start(f32[768]{0:T(1024)} %param.47) | copy-start | bytes 9220
  40.3 269.7 %all-reduce.7.cloned.1.call-start = ((), (), s32[]{:S(2)}) async-start(), calls=%async_computation.13 | async-start | bytes 6291456 | tf_op jit(solution)/shard_map/psum | solution.py:169
  168.1 141.9 %copy-start.63 = (f32[1024]{0:T(1024)}, f32[1024]{0:T(1024)S(1)}, u32[]{:S(2)}) copy-start(f32[1024]{0:T(1024)S(1)} %fusion.94) | copy-start | bytes 12292
  186.4 123.6 %copy-start.66 = (f32[768]{0:T(1024)S(1)}, f32[768]{0:T(1024)}, u32[]{:S(2)}) copy-start(f32[768]{0:T(1024)} %param.48) | copy-start | bytes 9220
  186.4 123.6 %copy-start.84 = (f32[768]{0:T(1024)S(1)}, f32[768]{0:T(1024)}, u32[]{:S(2)}) copy-start(f32[768]{0:T(1024)} %param.49) | copy-start | bytes 9220
  186.4 123.6 %copy-start.93 = (f32[768]{0:T(1024)S(1)}, f32[768]{0:T(1024)}, u32[]{:S(2)}) copy-start(f32[768]{0:T(1024)} %param.56) | copy-start | bytes 9220
  189.8 260.7 %all-reduce.9.cloned.1.call-start = ((), (), s32[]{:S(2)}) async-start(), calls=%async_computation.14 | async-start | bytes 6291456 | tf_op jit(solution)/shard_map/psum | solution.py:169
  313.9 387.0 %copy-start.61 = (f32[1024]{0:T(1024)}, f32[1024]{0:T(1024)S(1)}, u32[]{:S(2)}) copy-start(f32[1024]{0:T(1024)S(1)} %broadcast_multiply_fusion.1) | copy-start | bytes 12292
  316.1 134.3 %copy-start.68 = (f32[1024]{0:T(1024)}, f32[1024]{0:T(1024)S(1)}, u32[]{:S(2)}) copy-start(f32[1024]{0:T(1024)S(1)} %fusion.95) | copy-start | bytes 12292
  330.2 357.8 %all-gather.5.cloned.1.call-start = ((), (), s32[]{:S(2)}) async-start(), calls=%async_computation.19 | async-start | bytes 15728640 | tf_op jit(solution)/shard_map/all_gather | solution.py:172
  470.6 482.3 %all-gather.7.cloned.1.call-start = ((), (), s32[]{:S(2)}) async-start(), calls=%async_computation.20 | async-start | bytes 15728640 | tf_op jit(solution)/shard_map/all_gather | solution.py:172
  736.4 309.5 %reduce-scatter.51.cloned.1.call-start = ((), (), s32[]{:S(2)}) async-start(), calls=%async_computation.28 | async-start | bytes 884736
  739.8 311.9 %reduce-scatter.29.cloned.1.call-start = ((), (), s32[]{:S(2)}) async-start(), calls=%async_computation.15 | async-start | bytes 3932160 | tf_op jit(solution)/shard_map/reduce_scatter | solution.py:175
  745.0 345.0 %reduce-scatter.45.cloned.1.call-start = ((), (), s32[]{:S(2)}) async-start(), calls=%async_computation.25 | async-start | bytes 884736
  1003.1 149.4 %reduce-scatter.37.cloned.1.call-start = ((), (), s32[]{:S(2)}) async-start(), calls=%async_computation.21 | async-start | bytes 3932160
  1008.4 190.4 %reduce-scatter.35.cloned.1.call-start = ((), (), s32[]{:S(2)}) async-start(), calls=%async_computation.18 | async-start | bytes 2654208 | tf_op jit(solution)/shard_map/reduce_scatter | solution.py:309
  1014.1 231.5 %reduce-scatter.33.cloned.1.call-start = ((), (), s32[]{:S(2)}) async-start(), calls=%async_computation.17 | async-start | bytes 2654208 | tf_op jit(solution)/shard_map/reduce_scatter | solution.py:308
  1019.9 264.3 %reduce-scatter.31.cloned.1.call-start = ((), (), s32[]{:S(2)}) async-start(), calls=%async_computation.16 | async-start | bytes 884736 | tf_op jit(solution)/shard_map/reduce_scatter | solution.py:304
  1022.5 300.5 %reduce-scatter.49.cloned.1.call-start = ((), (), s32[]{:S(2)}) async-start(), calls=%async_computation.27 | async-start | bytes 884736
  1027.2 334.3 %reduce-scatter.47.cloned.1.call-start = ((), (), s32[]{:S(2)}) async-start(), calls=%async_computation.26 | async-start | bytes 884736
  1031.9 368.3 %reduce-scatter.43.cloned.1.call-start = ((), (), s32[]{:S(2)}) async-start(), calls=%async_computation.24 | async-start | bytes 884736
  1035.5 403.3 %reduce-scatter.39.cloned.1.call-start = ((), (), s32[]{:S(2)}) async-start(), calls=%async_computation.22 | async-start | bytes 884736
  1040.2 437.2 %reduce-scatter.41.cloned.1.call-start = ((), (), s32[]{:S(2)}) async-start(), calls=%async_computation.23 | async-start | bytes 884736
  (119 other events, 625.6 us)
Sparse Core Ops, SparseCore 0:
  40.4 123.7 all-reduce.4
  189.9 120.0 all-reduce.6
  330.3 120.0 all-reduce.8
  470.8 217.2 all-gather.4
  736.5 216.3 all-gather.6
  955.9 33.2 reduce-scatter.50
  991.5 60.2 reduce-scatter.28
  1054.9 35.0 reduce-scatter.44
  1092.3 60.2 reduce-scatter.36
  1156.3 42.4 reduce-scatter.34
  1203.1 42.4 reduce-scatter.32
  1249.2 34.9 reduce-scatter.30
  1288.0 34.9 reduce-scatter.48
  1326.6 34.9 reduce-scatter.46
  1365.2 34.9 reduce-scatter.42
  1403.8 34.9 reduce-scatter.38
  1442.4 34.9 reduce-scatter.40
